TPU v7x, 128 devices: a whole 4x4x4 slice. The times are simulated.
128 devices in a mesh: clip: 2 (over core), tm: 16 (over z, x), head: 4 (over y).
Axes of the slice: x: 4, y: 4, z: 4, core: 2. Of those that a mesh axis runs over, the one named last changes fastest.
Arguments:
- video_tokens: bfloat16 [64, 1568, 1024], P(('clip', 'tm')), parts along dimension 0, may hold values from -6 to 6
- window_order: int32 [64, 1568], P(('clip', 'tm')), parts along dimension 0, may hold values from 0 to 1567, each once within a row
- clip_id: int32 [64], P(('clip', 'tm')), parts along dimension 0, may hold values from 0 to 7, never falling along the last dimension, each value on 1 to 8 neighbouring positions
- attend_weight: bfloat16 [3, 1024, 1024], P(None, None, 'head'), may hold values from -0.75 to 0.75
- attend_out: bfloat16 [1024, 1024], P('head'), may hold values from -0.1875 to 0.1875
- recur_weight: bfloat16 [3, 1024, 1024], P(None, None, 'head'), may hold values from -0.1875 to 0.1875
- frame_decay: float32 [64, 1024], P(('clip', 'tm'), 'head'), parts along dimension 0, may hold values from -5.7 to -0.010625, as said below
- recur_out: bfloat16 [1024, 1024], P('head'), may hold values from -0.1875 to 0.1875
Outputs:
- features_out: bfloat16 [64, 1568, 1024], P(('clip', 'tm'), None, 'head'), parts along dimension 0
There are 2 independent parts, one for each index of `clip`. A program takes and returns all parts, laid end to end along the dimension named above; an argument that names none is the same for every part. Nothing has to cross between parts.
Inputs may be any that keep to these rules, and one draw needn't show every extreme that they name: `clip_id`: never falls along the frames; a clip spans 1 to 8 frames. `frame_decay`: negative.
All inputs are finite; a program needn't handle non-finite values.
Results may differ from a plain program's by a relative error of at most 0.01.
Values may be sent and summed in bfloat16 or wider, within the bound.
No kernel may reach another device: no remote copies, remote signals or barrier semaphores. Data moves between devices by JAX's collectives and lax.ppermute only.
A program may use at most 128 MiB of HBM per device.

v0:
```python
import jax
import jax.numpy as jnp
from jax import lax
from jax.sharding import PartitionSpec as P

HEAD_DIMENSION = 64
WINDOW = 49
EPSILON = 1e-06


def from_behind(value, axis, steps):
    count = lax.axis_size(axis)
    leading, last = (max(0, -steps), min(count, count - steps))
    return lax.ppermute(value, axis, [(source, source + steps) for source in range(leading, last)])


def normalize(values):
    return values * lax.rsqrt(jnp.mean(values * values, axis=-1, keepdims=True) + EPSILON)


def window_attention(queries, keys_all, values_all, window_order):
    frame_count, positions, number_of_heads, head_size = queries.shape
    order_index = window_order[:, :, None, None]

    def arrange(tensor):
        reordered = jnp.take_along_axis(tensor, order_index, axis=1)
        return reordered.reshape(
            frame_count, positions // WINDOW, WINDOW, number_of_heads, head_size
        )

    scores = jnp.einsum(
        "fwihe,fwjhe->fwhij",
        arrange(queries),
        arrange(keys_all),
        preferred_element_type=jnp.float32,
    ) / jnp.sqrt(jnp.float32(head_size))
    weights = jax.nn.softmax(scores, axis=-1).astype(jnp.bfloat16)
    blended = jnp.einsum(
        "fwhij,fwjhe->fwihe", weights, arrange(values_all), preferred_element_type=jnp.float32
    ).astype(jnp.bfloat16)
    blended = blended.reshape(frame_count, positions, number_of_heads, head_size)
    inverse = jnp.argsort(window_order, axis=1)
    return jnp.take_along_axis(blended, inverse[:, :, None, None], axis=1)


def per_device(
    video_tokens,
    window_order,
    clip_id,
    attend_weight,
    attend_out,
    recur_weight,
    frame_decay,
    recur_out,
):
    frame_count, positions, model_width = video_tokens.shape
    local_width = attend_weight.shape[2]
    row_count = frame_count * positions
    inputs = video_tokens.reshape(row_count, model_width).astype(jnp.float32)
    normed = normalize(inputs).astype(jnp.bfloat16)
    projected = jnp.einsum(
        "td,kde->kte", normed, attend_weight, preferred_element_type=jnp.float32
    ).astype(jnp.bfloat16)
    shaped = projected.reshape(
        3, frame_count, positions, local_width // HEAD_DIMENSION, HEAD_DIMENSION
    )
    attended = window_attention(shaped[0], shaped[1], shaped[2], window_order).reshape(
        row_count, local_width
    )
    partial_mix = jnp.dot(attended, attend_out, preferred_element_type=jnp.float32)
    offset = lax.axis_index("head") * local_width
    residual = inputs + lax.psum(partial_mix.astype(jnp.bfloat16), "head").astype(jnp.float32)
    normed_again = normalize(residual).astype(jnp.bfloat16)
    recur_proj = jnp.einsum(
        "td,kde->kte", normed_again, recur_weight, preferred_element_type=jnp.float32
    )
    residual_own = lax.dynamic_slice_in_dim(residual, offset, local_width, 1)
    gate_in = jax.nn.sigmoid(recur_proj[0]).reshape(frame_count, positions, local_width)
    value_in = recur_proj[1].reshape(frame_count, positions, local_width)
    out_gate = jax.nn.silu(recur_proj[2]).reshape(frame_count, positions, local_width)
    retain = jnp.exp(frame_decay)
    driven = jnp.sqrt(1.0 - retain * retain)[:, None, :] * gate_in * value_in
    previous = from_behind(clip_id[frame_count - 1 :], "tm", 1)
    continues = jnp.concatenate(
        [
            (clip_id[:1] == previous).astype(jnp.float32),
            (clip_id[1:] == clip_id[:-1]).astype(jnp.float32),
        ]
    )
    factor = retain * continues[:, None]

    def advance(carried, inputs_now):
        decay_total, state_now = carried
        factor_now, driven_now = inputs_now
        decay_total = factor_now * decay_total
        state_now = factor_now[None, :] * state_now + driven_now
        return ((decay_total, state_now), (decay_total, state_now))

    start_carry = (
        jnp.ones((local_width,), jnp.float32),
        jnp.zeros((positions, local_width), jnp.float32),
    )
    last_carry, all_carry = lax.scan(advance, start_carry, (factor, driven))
    decay_last, state_last = last_carry
    decay_all, state_all = all_carry

    def relay_step(counter, incoming):
        outgoing = decay_last[None, :] * incoming + state_last
        return from_behind(outgoing.astype(jnp.bfloat16), "tm", 1).astype(outgoing.dtype)

    incoming = lax.fori_loop(
        0, lax.axis_size("tm") - 1, relay_step, jnp.zeros((positions, local_width), jnp.float32)
    )
    states = state_all + decay_all[:, None, :] * incoming[None, :, :]
    output_rows = (states * out_gate).astype(jnp.bfloat16).reshape(row_count, local_width)
    partial_out = jnp.dot(output_rows, recur_out, preferred_element_type=jnp.float32)
    result = residual_own + lax.psum_scatter(
        partial_out.astype(jnp.bfloat16), "head", scatter_dimension=1, tiled=True
    ).astype(jnp.float32)
    return result.astype(jnp.bfloat16).reshape(frame_count, positions, local_width)


def solution(mesh):
    return jax.shard_map(
        per_device,
        mesh=mesh,
        in_specs=(
            P(("clip", "tm"), None, None),
            P(("clip", "tm"), None),
            P(("clip", "tm")),
            P(None, None, "head"),
            P("head", None),
            P(None, None, "head"),
            P(("clip", "tm"), "head"),
            P("head", None),
        ),
        out_specs=P(("clip", "tm"), None, "head"),
        check_vma=False,
    )
```

profile of v0, /device:TPU:1, one launch (start us, length us, event | category | flops | bytes accessed | tf_op | source)
XLA Modules:
  0.0 906.6 jit_solution(7665723979493977932)
XLA Ops:
  8.1 6.5 sort.17
  14.7 4.2 fusion.3
  19.0 3.9 fusion.4
  22.9 5.4 fusion.10
  33.3 28.2 %gather_fusion = bf16[3136,4,64]{2,1,0:T(4,128)(2,1)} fusion(bf16[2,1568,4,64]{3,2,1,0:T(4,128)(2,1)} %reshape.168, s32[3136]{0:T(1024)S(1)} %reshape.147), kind=kCustom, calls=%fused_computation.clone | custom fusion | bytes 3236352 | tf_op jit(solution)/shard_map/jit(take_along_axis)/gather | solution.py:26
  61.5 8.5 copy.39
  69.9 5.9 reshape.170
  75.9 37.3 %gather_fusion.1 = bf16[3136,4,64]{2,1,0:T(4,128)(2,1)} fusion(bf16[2,1568,4,64]{3,2,1,0:T(4,128)(2,1)} %reshape.170, s32[3136]{0:T(1024)S(1)} %reshape.147), kind=kCustom, calls=%fused_computation.1.clone | custom fusion | bytes 3236352 | tf_op jit(solution)/shard_map/jit(take_along_axis)/gather | solution.py:26
  113.2 9.4 %copy.43 = bf16[2,1568,4,64]{1,0,3,2:T(2,128)(2,1)} copy(bf16[2,1568,4,64]{3,2,1,0:T(4,128)(2,1)} %bitcast.90) | data formatting | bytes 3211264 | tf_op jit(solution)/shard_map/jit(take_along_axis)/gather | solution.py:26
  122.6 5.9 reshape.172
  128.5 28.5 %gather_fusion.2 = bf16[3136,4,64]{2,1,0:T(4,128)(2,1)} fusion(bf16[2,1568,4,64]{3,2,1,0:T(4,128)(2,1)} %reshape.172, s32[3136]{0:T(1024)S(1)} %reshape.147), kind=kCustom, calls=%fused_computation.2.clone | custom fusion | bytes 3236352 | tf_op jit(solution)/shard_map/jit(take_along_axis)/gather | solution.py:26
  157.0 9.3 %copy.47 = bf16[2,1568,4,64]{1,0,3,2:T(2,128)(2,1)} copy(bf16[2,1568,4,64]{3,2,1,0:T(4,128)(2,1)} %bitcast.87) | data formatting | bytes 3211264 | tf_op jit(solution)/shard_map/jit(take_along_axis)/gather | solution.py:26
  166.3 7.0 broadcast_select_fusion.3
  173.3 15.7 %reshape.171 = bf16[2,32,49,4,64]{2,1,0,4,3:T(8,128)(2,1)} reshape(bf16[2,1568,4,64]{1,0,3,2:T(2,128)(2,1)} %get-tuple-element.145) | data formatting | bytes 3211264 | tf_op jit(solution)/shard_map/reshape | solution.py:27
  189.0 14.4 %reshape.173 = bf16[2,32,49,4,64]{2,1,0,4,3:T(8,128)(2,1)} reshape(bf16[2,1568,4,64]{1,0,3,2:T(2,128)(2,1)S(1)} %copy-done.3) | data formatting | bytes 3211264 | tf_op jit(solution)/shard_map/reshape | solution.py:27
  203.3 15.2 %fusion.15 = f32[2,32,4,49,49]{3,4,2,1,0:T(8,128)S(1)} fusion(bf16[2,32,49,4,64]{2,1,0,4,3:T(8,128)(2,1)} %reshape.173, bf16[2,32,49,4,64]{2,1,0,4,3:T(8,128)(2,1)} %reshape.171), kind=kOutput, calls=%fused_computation.32 | convolution fusion | flops 78675968 | bytes 5669888 | tf_op jit(solution)/shard_map/fwihe,fwjhe->fwhij/dot_general | solution.py:31
  218.6 5.5 fusion.30
  224.1 14.4 %reshape.169 = bf16[2,32,49,4,64]{2,1,0,4,3:T(8,128)(2,1)} reshape(bf16[2,1568,4,64]{1,0,3,2:T(2,128)(2,1)S(1)} %copy-done.2) | data formatting | bytes 3211264 | tf_op jit(solution)/shard_map/reshape | solution.py:27
  238.5 13.6 %convert_bitcast_fusion = bf16[2,32,49,4,64]{4,2,3,1,0:T(8,128)(2,1)S(1)} fusion(f32[2,32,4,49,49]{3,4,2,1,0:T(8,128)} %get-tuple-element.152, f32[2,32,4,49]{3,2,1,0:T(4,128)S(1)} %get-tuple-element.151, bf16[2,32,49,4,64]{2,1,0,4,3:T(8,128)(2,1)} %reshape.169), kind=kOutput, calls=%fused_computation.37 | convolution fusion | flops 80708096 | bytes 5720064 | tf_op jit(solution)/shard_map/fwhij,fwjhe->fwihe/dot_general | solution.py:38
  255.1 28.3 %gather_fusion.3 = bf16[3136,4,64]{2,1,0:T(4,128)(2,1)} fusion(bf16[2,1568,4,64]{3,2,1,0:T(4,128)(2,1)} %bitcast.91, s32[3136]{0:T(1024)S(1)} %reshape.162), kind=kCustom, calls=%fused_computation.3.clone | custom fusion | bytes 3236352 | tf_op jit(solution)/shard_map/jit(take_along_axis)/gather | solution.py:43
  283.4 8.5 copy.36
  298.3 4.6 convolution_convert_fusion.1
  304.1 4.5 collective-permute-start.1
  311.2 124.0 %all-reduce.2.cloned.1.call-done = bf16[3136,1024]{1,0:T(8,128)(2,1)} async-done(((bf16[3136,1024]{1,0:T(8,128)(2,1)}), bf16[3136,1024]{1,0:T(8,128)(2,1)}) %all-reduce.2.cloned.1.call-update) | async-done | bytes 6422544 | tf_op jit(solution)/shard_map/psum | solution.py:72
  435.2 12.4 %bitcast_add_fusion.1 = f32[3136,1024]{1,0:T(8,128)} fusion(bf16[2,1568,1024]{2,1,0:T(8,128)(2,1)} %param.14, bf16[3136,1024]{1,0:T(8,128)(2,1)} %all-reduce.2.cloned.1.call-done), kind=kLoop, calls=%fused_computation.13 | loop fusion | flops 9633792 | bytes 25690112 | tf_op jit(solution)/shard_map/add | solution.py:72
  447.6 5.7 multiply_reduce_fusion
  453.3 11.2 %convolution_bitcast_fusion = f32[3,3136,256]{2,1,0:T(8,128)} fusion(bf16[3,1024,256]{2,1,0:T(8,128)(2,1)S(1)} %copy-done.8, f32[3136,1024]{1,0:T(8,128)} %bitcast_add_fusion.1, f32[3136]{0:T(1024)S(1)} %add_rsqrt_fusion), kind=kOutput, calls=%fused_computation.20 | convolution fusion | flops 4938924032 | bytes 24064256 | tf_op jit(solution)/shard_map/td,kde->kte/dot_general | solution.py:74
  464.5 6.3 fusion.24
  472.9 6.5 while.28
  479.4 315.5 %while.29 = (s32[]{:T(128)}, f32[1568,256]{1,0:T(8,128)}, f32[256]{0:T(256)S(1)}, f32[1568,256]{1,0:T(8,128)S(1)}, s32[]{:T(128)}, /*index=5*/s32[]{:T(128)}) while((s32[]{:T(128)}, f32[1568,256]{1,0:T(8,128)}, f32[256]{0:T(256)S(1)}, f32[1568,256]{1,0:T(8,128)S(1)}, s32[]{:T(128)}, /*index=5*/s32[]{:T(128)}) %tuple.55), condition=%wide.region_9.11_spmd.clone, body=%wide.region_8.10_spmd.clone.sunk | while | flops 2007043 | bytes 9634935 | solution.py:111
  479.7 4.1 collective-permute-start
  483.7 15.5 %collective-permute-done = bf16[1568,256]{1,0:T(8,128)(2,1)} collective-permute-done((bf16[1568,256]{1,0:T(8,128)(2,1)S(1)}, bf16[1568,256]{1,0:T(8,128)(2,1)}, u32[]{:S(2)}, u32[]{:S(2)}) %collective-permute-start) | collective-permute-done | bytes 802848 | tf_op jit(solution)/shard_map/while/body/eval_jaxpr/ppermute | solution.py:14
  503.4 5.2 collective-permute-start
  508.5 14.6 %collective-permute-done = bf16[1568,256]{1,0:T(8,128)(2,1)} collective-permute-done((bf16[1568,256]{1,0:T(8,128)(2,1)S(1)}, bf16[1568,256]{1,0:T(8,128)(2,1)}, u32[]{:S(2)}, u32[]{:S(2)}) %collective-permute-start) | collective-permute-done | bytes 802848 | tf_op jit(solution)/shard_map/while/body/eval_jaxpr/ppermute | solution.py:14
  527.2 5.2 collective-permute-start
  532.4 13.7 %collective-permute-done = bf16[1568,256]{1,0:T(8,128)(2,1)} collective-permute-done((bf16[1568,256]{1,0:T(8,128)(2,1)S(1)}, bf16[1568,256]{1,0:T(8,128)(2,1)}, u32[]{:S(2)}, u32[]{:S(2)}) %collective-permute-start) | collective-permute-done | bytes 802848 | tf_op jit(solution)/shard_map/while/body/eval_jaxpr/ppermute | solution.py:14
  550.2 5.2 collective-permute-start
  555.3 12.8 %collective-permute-done = bf16[1568,256]{1,0:T(8,128)(2,1)} collective-permute-done((bf16[1568,256]{1,0:T(8,128)(2,1)S(1)}, bf16[1568,256]{1,0:T(8,128)(2,1)}, u32[]{:S(2)}, u32[]{:S(2)}) %collective-permute-start) | collective-permute-done | bytes 802848 | tf_op jit(solution)/shard_map/while/body/eval_jaxpr/ppermute | solution.py:14
  572.2 5.2 collective-permute-start
  577.3 11.9 %collective-permute-done = bf16[1568,256]{1,0:T(8,128)(2,1)} collective-permute-done((bf16[1568,256]{1,0:T(8,128)(2,1)S(1)}, bf16[1568,256]{1,0:T(8,128)(2,1)}, u32[]{:S(2)}, u32[]{:S(2)}) %collective-permute-start) | collective-permute-done | bytes 802848 | tf_op jit(solution)/shard_map/while/body/eval_jaxpr/ppermute | solution.py:14
  593.3 5.8 collective-permute-start
  599.0 10.9 %collective-permute-done = bf16[1568,256]{1,0:T(8,128)(2,1)} collective-permute-done((bf16[1568,256]{1,0:T(8,128)(2,1)S(1)}, bf16[1568,256]{1,0:T(8,128)(2,1)}, u32[]{:S(2)}, u32[]{:S(2)}) %collective-permute-start) | collective-permute-done | bytes 802848 | tf_op jit(solution)/shard_map/while/body/eval_jaxpr/ppermute | solution.py:14
  614.0 7.3 collective-permute-start
  621.3 10.0 %collective-permute-done = bf16[1568,256]{1,0:T(8,128)(2,1)} collective-permute-done((bf16[1568,256]{1,0:T(8,128)(2,1)S(1)}, bf16[1568,256]{1,0:T(8,128)(2,1)}, u32[]{:S(2)}, u32[]{:S(2)}) %collective-permute-start) | collective-permute-done | bytes 802848 | tf_op jit(solution)/shard_map/while/body/eval_jaxpr/ppermute | solution.py:14
  635.4 7.3 collective-permute-start
  642.7 9.1 %collective-permute-done = bf16[1568,256]{1,0:T(8,128)(2,1)} collective-permute-done((bf16[1568,256]{1,0:T(8,128)(2,1)S(1)}, bf16[1568,256]{1,0:T(8,128)(2,1)}, u32[]{:S(2)}, u32[]{:S(2)}) %collective-permute-start) | collective-permute-done | bytes 802848 | tf_op jit(solution)/shard_map/while/body/eval_jaxpr/ppermute | solution.py:14
  655.8 7.3 collective-permute-start
  663.1 8.1 collective-permute-done
  675.3 7.3 collective-permute-start
  682.6 8.1 collective-permute-done
  694.8 7.3 collective-permute-start
  702.1 8.1 collective-permute-done
  714.3 7.3 collective-permute-start
  721.6 8.1 collective-permute-done
  733.8 7.3 collective-permute-start
  741.1 8.4 collective-permute-done
  753.5 7.3 collective-permute-start
  760.8 9.5 %collective-permute-done = bf16[1568,256]{1,0:T(8,128)(2,1)} collective-permute-done((bf16[1568,256]{1,0:T(8,128)(2,1)S(1)}, bf16[1568,256]{1,0:T(8,128)(2,1)}, u32[]{:S(2)}, u32[]{:S(2)}) %collective-permute-start) | collective-permute-done | bytes 802848 | tf_op jit(solution)/shard_map/while/body/eval_jaxpr/ppermute | solution.py:14
  774.4 7.6 collective-permute-start
  781.9 10.6 %collective-permute-done = bf16[1568,256]{1,0:T(8,128)(2,1)} collective-permute-done((bf16[1568,256]{1,0:T(8,128)(2,1)S(1)}, bf16[1568,256]{1,0:T(8,128)(2,1)}, u32[]{:S(2)}, u32[]{:S(2)}) %collective-permute-start) | collective-permute-done | bytes 802848 | tf_op jit(solution)/shard_map/while/body/eval_jaxpr/ppermute | solution.py:14
  794.9 4.3 multiply_convert_fusion.1
  799.2 4.5 convolution_convert_fusion
  803.7 91.7 %reduce-scatter.2.cloned.1.call-done = bf16[3136,256]{1,0:T(8,128)(2,1)} async-done(((bf16[3136,1024]{1,0:T(8,128)(2,1)}), bf16[3136,256]{1,0:T(8,128)(2,1)}) %reduce-scatter.2.cloned.1.call-update) | async-done | bytes 1605648 | tf_op jit(solution)/shard_map/reduce_scatter | solution.py:117
  895.4 3.9 add_convert_fusion
  (85 shorter events, 85.5 us)
Async XLA Ops:
  6.5 16.3 %copy-start = (bf16[3,1024,256]{2,1,0:T(8,128)(2,1)S(1)}, bf16[3,1024,256]{2,1,0:T(8,128)(2,1)}, u32[]{:S(2)}) copy-start(bf16[3,1024,256]{2,1,0:T(8,128)(2,1)} %param.17) | copy-start | bytes 4718596
  6.5 428.7 %all-reduce.2.cloned.1.call-start = ((), (), s32[]{:S(2)}) async-start(), calls=%async_computation.1 | async-start | bytes 12845056 | tf_op jit(solution)/shard_map/psum | solution.py:72
  173.3 15.7 %copy-start.3 = (bf16[2,1568,4,64]{1,0,3,2:T(2,128)(2,1)S(1)}, bf16[2,1568,4,64]{1,0,3,2:T(2,128)(2,1)}, u32[]{:S(2)}) copy-start(bf16[2,1568,4,64]{1,0,3,2:T(2,128)(2,1)} %get-tuple-element.146) | copy-start | bytes 4816900
  218.6 5.5 copy-start.2
  291.9 6.4 copy-start.4
  302.8 0.7 copy-start.7
  302.8 8.3 copy-start.6
  302.9 592.5 %reduce-scatter.2.cloned.1.call-start = ((), (), s32[]{:S(2)}) async-start(), calls=%async_computation.2 | async-start | bytes 8028160 | tf_op jit(solution)/shard_map/reduce_scatter | solution.py:117
  304.1 5.7 collective-permute-start.1
  447.6 5.7 copy-start.8
  479.7 19.6 %collective-permute-start = (bf16[1568,256]{1,0:T(8,128)(2,1)S(1)}, bf16[1568,256]{1,0:T(8,128)(2,1)}, u32[]{:S(2)}, u32[]{:S(2)}) collective-permute-start(bf16[1568,256]{1,0:T(8,128)(2,1)S(1)} %fusion.38), channel_id=1, source_target_pairs={{0,4},{4,8},{8,12},{12,16},{16,20},{20,24},{24,28},{28,32},{32,36}... | collective-permute-start | bytes 2408456 | tf_op jit(solution)/shard_map/while/body/eval_jaxpr/ppermute | solution.py:14
  503.4 19.8 %collective-permute-start = (bf16[1568,256]{1,0:T(8,128)(2,1)S(1)}, bf16[1568,256]{1,0:T(8,128)(2,1)}, u32[]{:S(2)}, u32[]{:S(2)}) collective-permute-start(bf16[1568,256]{1,0:T(8,128)(2,1)S(1)} %fusion.38), channel_id=1, source_target_pairs={{0,4},{4,8},{8,12},{12,16},{16,20},{20,24},{24,28},{28,32},{32,36}... | collective-permute-start | bytes 2408456 | tf_op jit(solution)/shard_map/while/body/eval_jaxpr/ppermute | solution.py:14
  527.2 18.9 %collective-permute-start = (bf16[1568,256]{1,0:T(8,128)(2,1)S(1)}, bf16[1568,256]{1,0:T(8,128)(2,1)}, u32[]{:S(2)}, u32[]{:S(2)}) collective-permute-start(bf16[1568,256]{1,0:T(8,128)(2,1)S(1)} %fusion.38), channel_id=1, source_target_pairs={{0,4},{4,8},{8,12},{12,16},{16,20},{20,24},{24,28},{28,32},{32,36}... | collective-permute-start | bytes 2408456 | tf_op jit(solution)/shard_map/while/body/eval_jaxpr/ppermute | solution.py:14
  550.2 18.0 %collective-permute-start = (bf16[1568,256]{1,0:T(8,128)(2,1)S(1)}, bf16[1568,256]{1,0:T(8,128)(2,1)}, u32[]{:S(2)}, u32[]{:S(2)}) collective-permute-start(bf16[1568,256]{1,0:T(8,128)(2,1)S(1)} %fusion.38), channel_id=1, source_target_pairs={{0,4},{4,8},{8,12},{12,16},{16,20},{20,24},{24,28},{28,32},{32,36}... | collective-permute-start | bytes 2408456 | tf_op jit(solution)/shard_map/while/body/eval_jaxpr/ppermute | solution.py:14
  572.2 17.0 %collective-permute-start = (bf16[1568,256]{1,0:T(8,128)(2,1)S(1)}, bf16[1568,256]{1,0:T(8,128)(2,1)}, u32[]{:S(2)}, u32[]{:S(2)}) collective-permute-start(bf16[1568,256]{1,0:T(8,128)(2,1)S(1)} %fusion.38), channel_id=1, source_target_pairs={{0,4},{4,8},{8,12},{12,16},{16,20},{20,24},{24,28},{28,32},{32,36}... | collective-permute-start | bytes 2408456 | tf_op jit(solution)/shard_map/while/body/eval_jaxpr/ppermute | solution.py:14
  593.3 16.7 %collective-permute-start = (bf16[1568,256]{1,0:T(8,128)(2,1)S(1)}, bf16[1568,256]{1,0:T(8,128)(2,1)}, u32[]{:S(2)}, u32[]{:S(2)}) collective-permute-start(bf16[1568,256]{1,0:T(8,128)(2,1)S(1)} %fusion.38), channel_id=1, source_target_pairs={{0,4},{4,8},{8,12},{12,16},{16,20},{20,24},{24,28},{28,32},{32,36}... | collective-permute-start | bytes 2408456 | tf_op jit(solution)/shard_map/while/body/eval_jaxpr/ppermute | solution.py:14
  614.0 17.3 %collective-permute-start = (bf16[1568,256]{1,0:T(8,128)(2,1)S(1)}, bf16[1568,256]{1,0:T(8,128)(2,1)}, u32[]{:S(2)}, u32[]{:S(2)}) collective-permute-start(bf16[1568,256]{1,0:T(8,128)(2,1)S(1)} %fusion.38), channel_id=1, source_target_pairs={{0,4},{4,8},{8,12},{12,16},{16,20},{20,24},{24,28},{28,32},{32,36}... | collective-permute-start | bytes 2408456 | tf_op jit(solution)/shard_map/while/body/eval_jaxpr/ppermute | solution.py:14
  635.4 16.4 %collective-permute-start = (bf16[1568,256]{1,0:T(8,128)(2,1)S(1)}, bf16[1568,256]{1,0:T(8,128)(2,1)}, u32[]{:S(2)}, u32[]{:S(2)}) collective-permute-start(bf16[1568,256]{1,0:T(8,128)(2,1)S(1)} %fusion.38), channel_id=1, source_target_pairs={{0,4},{4,8},{8,12},{12,16},{16,20},{20,24},{24,28},{28,32},{32,36}... | collective-permute-start | bytes 2408456 | tf_op jit(solution)/shard_map/while/body/eval_jaxpr/ppermute | solution.py:14
  655.8 15.4 %collective-permute-start = (bf16[1568,256]{1,0:T(8,128)(2,1)S(1)}, bf16[1568,256]{1,0:T(8,128)(2,1)}, u32[]{:S(2)}, u32[]{:S(2)}) collective-permute-start(bf16[1568,256]{1,0:T(8,128)(2,1)S(1)} %fusion.38), channel_id=1, source_target_pairs={{0,4},{4,8},{8,12},{12,16},{16,20},{20,24},{24,28},{28,32},{32,36}... | collective-permute-start | bytes 2408456 | tf_op jit(solution)/shard_map/while/body/eval_jaxpr/ppermute | solution.py:14
  675.3 15.4 %collective-permute-start = (bf16[1568,256]{1,0:T(8,128)(2,1)S(1)}, bf16[1568,256]{1,0:T(8,128)(2,1)}, u32[]{:S(2)}, u32[]{:S(2)}) collective-permute-start(bf16[1568,256]{1,0:T(8,128)(2,1)S(1)} %fusion.38), channel_id=1, source_target_pairs={{0,4},{4,8},{8,12},{12,16},{16,20},{20,24},{24,28},{28,32},{32,36}... | collective-permute-start | bytes 2408456 | tf_op jit(solution)/shard_map/while/body/eval_jaxpr/ppermute | solution.py:14
  694.8 15.4 %collective-permute-start = (bf16[1568,256]{1,0:T(8,128)(2,1)S(1)}, bf16[1568,256]{1,0:T(8,128)(2,1)}, u32[]{:S(2)}, u32[]{:S(2)}) collective-permute-start(bf16[1568,256]{1,0:T(8,128)(2,1)S(1)} %fusion.38), channel_id=1, source_target_pairs={{0,4},{4,8},{8,12},{12,16},{16,20},{20,24},{24,28},{28,32},{32,36}... | collective-permute-start | bytes 2408456 | tf_op jit(solution)/shard_map/while/body/eval_jaxpr/ppermute | solution.py:14
  714.3 15.4 %collective-permute-start = (bf16[1568,256]{1,0:T(8,128)(2,1)S(1)}, bf16[1568,256]{1,0:T(8,128)(2,1)}, u32[]{:S(2)}, u32[]{:S(2)}) collective-permute-start(bf16[1568,256]{1,0:T(8,128)(2,1)S(1)} %fusion.38), channel_id=1, source_target_pairs={{0,4},{4,8},{8,12},{12,16},{16,20},{20,24},{24,28},{28,32},{32,36}... | collective-permute-start | bytes 2408456 | tf_op jit(solution)/shard_map/while/body/eval_jaxpr/ppermute | solution.py:14
  733.8 15.7 %collective-permute-start = (bf16[1568,256]{1,0:T(8,128)(2,1)S(1)}, bf16[1568,256]{1,0:T(8,128)(2,1)}, u32[]{:S(2)}, u32[]{:S(2)}) collective-permute-start(bf16[1568,256]{1,0:T(8,128)(2,1)S(1)} %fusion.38), channel_id=1, source_target_pairs={{0,4},{4,8},{8,12},{12,16},{16,20},{20,24},{24,28},{28,32},{32,36}... | collective-permute-start | bytes 2408456 | tf_op jit(solution)/shard_map/while/body/eval_jaxpr/ppermute | solution.py:14
  753.5 16.8 %collective-permute-start = (bf16[1568,256]{1,0:T(8,128)(2,1)S(1)}, bf16[1568,256]{1,0:T(8,128)(2,1)}, u32[]{:S(2)}, u32[]{:S(2)}) collective-permute-start(bf16[1568,256]{1,0:T(8,128)(2,1)S(1)} %fusion.38), channel_id=1, source_target_pairs={{0,4},{4,8},{8,12},{12,16},{16,20},{20,24},{24,28},{28,32},{32,36}... | collective-permute-start | bytes 2408456 | tf_op jit(solution)/shard_map/while/body/eval_jaxpr/ppermute | solution.py:14
  774.4 18.1 %collective-permute-start = (bf16[1568,256]{1,0:T(8,128)(2,1)S(1)}, bf16[1568,256]{1,0:T(8,128)(2,1)}, u32[]{:S(2)}, u32[]{:S(2)}) collective-permute-start(bf16[1568,256]{1,0:T(8,128)(2,1)S(1)} %fusion.38), channel_id=1, source_target_pairs={{0,4},{4,8},{8,12},{12,16},{16,20},{20,24},{24,28},{28,32},{32,36}... | collective-permute-start | bytes 2408456 | tf_op jit(solution)/shard_map/while/body/eval_jaxpr/ppermute | solution.py:14
  794.9 4.3 copy-start.5
  803.7 95.7 %copy-start.1 = (bf16[3,1024,256]{2,1,0:T(8,128)(2,1)S(1)}, bf16[3,1024,256]{2,1,0:T(8,128)(2,1)}, u32[]{:S(2)}) copy-start(bf16[3,1024,256]{2,1,0:T(8,128)(2,1)} %param.17) | copy-start | bytes 4718596
Sparse Core Ops, SparseCore 0:
  303.0 132.1 all-reduce.1
  803.8 91.5 reduce-scatter.1
where the time goes:
time: 916 us; the launch traced here: 907 us
  waiting for transfers between devices  375 us (41%)
  local copies, waits for them, and re-layouts  227 us (25%)
  other arithmetic  132 us (14%)
  starting transfers between devices  101 us (11%)
  matrix products  54.5 us (6%)
  between operations  16.5 us (2%)
    ppermute x16, waiting for transfers between devices, from_behind(): lax.ppermute(value, axis, [(source, source + steps) for source in range(l...  160 us
    psum x1, waiting for transfers between devices, per_device(): lax.psum(partial_mix.astype(jnp.bfloat16), 'head').astype(jnp.float32)  124 us
    gather x7, local copies, waits for them, and re-layouts, arrange(): reordered = jnp.take_along_axis(tensor, order_index, axis=1)  121 us
    ppermute x16, starting transfers between devices, from_behind(): lax.ppermute(value, axis, [(source, source + steps) for source in range(l...  101 us
    reduce_scatter x1, waiting for transfers between devices, per_device(): lax.psum_scatter(partial_out.astype(jnp.bfloat16), 'head', scatter_dimens...  91.7 us
    reshape x3, local copies, waits for them, and re-layouts, arrange(): reordered.reshape(frame_count, positions // WINDOW, WINDOW, number_of_hea...  44.4 us
    gather x3, local copies, waits for them, and re-layouts, window_attention(): return jnp.take_along_axis(blended, inverse[:, :, None, None], axis=1)  36.8 us
    convert_element_type x15, other arithmetic, relay_step(): from_behind(outgoing.astype(jnp.bfloat16), 'tm', 1).astype(outgoing.dtype)  36.2 us
  transfers between devices with their start and end apart: 18, of which 17 were waited for; matrix products, arithmetic and copies ran while one was open for 0% of the time, Pallas kernels for 0%

commit v1 on v0

--- a/solution.py
+++ b/solution.py
@@ -69,7 +69,8 @@
     )
     partial_mix = jnp.dot(attended, attend_out, preferred_element_type=jnp.float32)
     offset = lax.axis_index("head") * local_width
-    residual = inputs + lax.psum(partial_mix.astype(jnp.bfloat16), "head").astype(jnp.float32)
+    column_treat = lambda x_in, axis_tag: jnp.sum(lax.all_gather(x_in, axis_tag), axis=0)
+    residual = inputs + column_treat(partial_mix.astype(jnp.bfloat16), "head").astype(jnp.float32)
     normed_again = normalize(residual).astype(jnp.bfloat16)
     recur_proj = jnp.einsum(
         "td,kde->kte", normed_again, recur_weight, preferred_element_type=jnp.float32

time: 916 us -> 1040 us (1.14)
  waiting for transfers between devices: 375 us -> 475 us
  other arithmetic: 132 us -> 155 us
    all_gather x0 -> x1, waiting for transfers between devices: none -> 223 us  [per_device(): lax.all_gather(x_in, axis_tag)]
    psum x1 -> x0, waiting for transfers between devices: 124 us -> none  [per_device(): lax.psum(partial_mix.astype(jnp.bfloat16), 'head').astype(jnp.float32)]
    reduce_sum x0 -> x1, other arithmetic: none -> 21.4 us  [per_device(): jnp.sum(lax.all_gather(x_in, axis_tag), axis=0)]
where the time goes in v1:
time: 1040 us; the launch traced here: 1030 us
  waiting for transfers between devices  475 us (46%)
  local copies, waits for them, and re-layouts  227 us (22%)
  other arithmetic  155 us (15%)
  starting transfers between devices  101 us (10%)
  matrix products  54.7 us (5%)
  between operations  16.5 us (2%)
    all_gather x1, waiting for transfers between devices, per_device(): lax.all_gather(x_in, axis_tag)  223 us
    ppermute x16, waiting for transfers between devices, from_behind(): lax.ppermute(value, axis, [(source, source + steps) for source in range(l...  160 us
    gather x7, local copies, waits for them, and re-layouts, arrange(): reordered = jnp.take_along_axis(tensor, order_index, axis=1)  121 us
    ppermute x16, starting transfers between devices, from_behind(): lax.ppermute(value, axis, [(source, source + steps) for source in range(l...  101 us
    reduce_scatter x1, waiting for transfers between devices, per_device(): lax.psum_scatter(partial_out.astype(jnp.bfloat16), 'head', scatter_dimens...  92.4 us
    reshape x3, local copies, waits for them, and re-layouts, arrange(): reordered.reshape(frame_count, positions // WINDOW, WINDOW, number_of_hea...  44.4 us
    gather x3, local copies, waits for them, and re-layouts, window_attention(): return jnp.take_along_axis(blended, inverse[:, :, None, None], axis=1)  36.9 us
    convert_element_type x15, other arithmetic, relay_step(): from_behind(outgoing.astype(jnp.bfloat16), 'tm', 1).astype(outgoing.dtype)  36.2 us
  transfers between devices with their start and end apart: 18, of which 17 were waited for; matrix products, arithmetic and copies ran while one was open for 0% of the time, Pallas kernels for 0%

profile of v1, /device:TPU:1, one launch (start us, length us, event | category | flops | bytes accessed | tf_op | source)
XLA Modules:
  0.0 1029.8 jit_solution(10926681339691768028)
XLA Ops:
  8.1 6.5 sort.17
  14.7 4.2 fusion.3
  22.9 5.4 fusion.12
  33.3 28.2 %gather_fusion = bf16[3136,4,64]{2,1,0:T(4,128)(2,1)} fusion(bf16[2,1568,4,64]{3,2,1,0:T(4,128)(2,1)} %reshape.182, s32[3136]{0:T(1024)S(1)} %reshape.161), kind=kCustom, calls=%fused_computation.clone | custom fusion | bytes 3236352 | tf_op jit(solution)/shard_map/jit(take_along_axis)/gather | solution.py:26
  61.5 8.5 copy.39
  69.9 6.0 reshape.184
  75.9 37.3 %gather_fusion.1 = bf16[3136,4,64]{2,1,0:T(4,128)(2,1)} fusion(bf16[2,1568,4,64]{3,2,1,0:T(4,128)(2,1)} %reshape.184, s32[3136]{0:T(1024)S(1)} %reshape.161), kind=kCustom, calls=%fused_computation.1.clone | custom fusion | bytes 3236352 | tf_op jit(solution)/shard_map/jit(take_along_axis)/gather | solution.py:26
  113.2 9.4 copy.43
  122.6 5.9 reshape.186
  128.5 28.5 %gather_fusion.2 = bf16[3136,4,64]{2,1,0:T(4,128)(2,1)} fusion(bf16[2,1568,4,64]{3,2,1,0:T(4,128)(2,1)} %reshape.186, s32[3136]{0:T(1024)S(1)} %reshape.161), kind=kCustom, calls=%fused_computation.2.clone | custom fusion | bytes 3236352 | tf_op jit(solution)/shard_map/jit(take_along_axis)/gather | solution.py:26
  157.0 9.3 copy.47
  166.3 7.0 broadcast_select_fusion.3
  173.3 15.7 %reshape.185 = bf16[2,32,49,4,64]{2,1,0,4,3:T(8,128)(2,1)} reshape(bf16[2,1568,4,64]{1,0,3,2:T(2,128)(2,1)} %get-tuple-element.145) | data formatting | bytes 3211264 | tf_op jit(solution)/shard_map/reshape | solution.py:27
  189.0 14.4 %reshape.187 = bf16[2,32,49,4,64]{2,1,0,4,3:T(8,128)(2,1)} reshape(bf16[2,1568,4,64]{1,0,3,2:T(2,128)(2,1)S(1)} %copy-done.3) | data formatting | bytes 3211264 | tf_op jit(solution)/shard_map/reshape | solution.py:27
  203.4 15.2 %fusion.17 = f32[2,32,4,49,49]{3,4,2,1,0:T(8,128)S(1)} fusion(bf16[2,32,49,4,64]{2,1,0,4,3:T(8,128)(2,1)} %reshape.187, bf16[2,32,49,4,64]{2,1,0,4,3:T(8,128)(2,1)} %reshape.185), kind=kOutput, calls=%fused_computation.34 | convolution fusion | flops 78675968 | bytes 5669888 | tf_op jit(solution)/shard_map/fwihe,fwjhe->fwhij/dot_general | solution.py:31
  218.6 5.5 fusion.32
  224.1 14.4 %reshape.183 = bf16[2,32,49,4,64]{2,1,0,4,3:T(8,128)(2,1)} reshape(bf16[2,1568,4,64]{1,0,3,2:T(2,128)(2,1)S(1)} %copy-done.2) | data formatting | bytes 3211264 | tf_op jit(solution)/shard_map/reshape | solution.py:27
  238.5 13.6 %convert_bitcast_fusion = bf16[2,32,49,4,64]{4,2,3,1,0:T(8,128)(2,1)S(1)} fusion(f32[2,32,4,49,49]{3,4,2,1,0:T(8,128)} %get-tuple-element.152, f32[2,32,4,49]{3,2,1,0:T(4,128)S(1)} %get-tuple-element.151, bf16[2,32,49,4,64]{2,1,0,4,3:T(8,128)(2,1)} %reshape.183), kind=kOutput, calls=%fused_computation.39 | convolution fusion | flops 80708096 | bytes 5720064 | tf_op jit(solution)/shard_map/fwhij,fwjhe->fwihe/dot_general | solution.py:38
  255.1 28.3 %gather_fusion.3 = bf16[3136,4,64]{2,1,0:T(4,128)(2,1)} fusion(bf16[2,1568,4,64]{3,2,1,0:T(4,128)(2,1)} %bitcast.96, s32[3136]{0:T(1024)S(1)} %reshape.176), kind=kCustom, calls=%fused_computation.3.clone | custom fusion | bytes 3236352 | tf_op jit(solution)/shard_map/jit(take_along_axis)/gather | solution.py:43
  283.4 8.5 copy.36
  298.3 4.6 convolution_convert_fusion.1
  304.1 4.5 collective-permute-start.1
  311.2 223.2 %all-gather.3.cloned.1.call-done = bf16[12544,1024]{1,0:T(8,128)(2,1)} async-done(((bf16[3136,1024]{1,0:T(8,128)(2,1)}), bf16[12544,1024]{1,0:T(8,128)(2,1)}) %all-gather.3.cloned.1.call-update) | async-done | bytes 25690128 | tf_op jit(solution)/shard_map/all_gather | solution.py:72
  534.4 21.4 %reduce_sum.41 = bf16[3136,1024]{1,0:T(8,128)(2,1)} reduce(bf16[4,3136,1024]{2,1,0:T(8,128)(2,1)} %bitcast.88, bf16[]{:T(256)} %constant.34.clone.1), dimensions={0}, to_apply=%region_4.0 | reduce | flops 9633792 | bytes 32112642 | tf_op jit(solution)/shard_map/reduce_sum | solution.py:72
  555.9 12.4 %bitcast_add_fusion.1 = f32[3136,1024]{1,0:T(8,128)} fusion(bf16[2,1568,1024]{2,1,0:T(8,128)(2,1)} %param.14, bf16[3136,1024]{1,0:T(8,128)(2,1)} %reduce_sum.41), kind=kLoop, calls=%fused_computation.13 | loop fusion | flops 9633792 | bytes 25690112 | tf_op jit(solution)/shard_map/add | solution.py:73
  568.2 6.8 fusion.5
  575.2 11.4 %convolution_bitcast_fusion = f32[3,3136,256]{2,1,0:T(8,128)} fusion(bf16[3,1024,256]{2,1,0:T(8,128)(2,1)} %param.19, f32[3136,1024]{1,0:T(8,128)} %bitcast_add_fusion.1, f32[3136]{0:T(1024)S(1)} %rsqrt.25), kind=kOutput, calls=%fused_computation.22 | convolution fusion | flops 4938924032 | bytes 24064256 | tf_op jit(solution)/shard_map/td,kde->kte/dot_general | solution.py:75
  586.5 6.3 fusion.26
  595.0 6.5 while.28
  601.4 316.0 %while.29 = (s32[]{:T(128)}, f32[1568,256]{1,0:T(8,128)}, f32[256]{0:T(256)S(1)}, f32[1568,256]{1,0:T(8,128)S(1)}, s32[]{:T(128)}, /*index=5*/s32[]{:T(128)}) while((s32[]{:T(128)}, f32[1568,256]{1,0:T(8,128)}, f32[256]{0:T(256)S(1)}, f32[1568,256]{1,0:T(8,128)S(1)}, s32[]{:T(128)}, /*index=5*/s32[]{:T(128)}) %tuple.55), condition=%wide.region_9.11_spmd.clone, body=%wide.region_8.10_spmd.clone.sunk | while | flops 2007043 | bytes 9634935 | solution.py:112
  601.9 4.1 collective-permute-start
  606.0 15.6 %collective-permute-done = bf16[1568,256]{1,0:T(8,128)(2,1)} collective-permute-done((bf16[1568,256]{1,0:T(8,128)(2,1)S(1)}, bf16[1568,256]{1,0:T(8,128)(2,1)}, u32[]{:S(2)}, u32[]{:S(2)}) %collective-permute-start) | collective-permute-done | bytes 802848 | tf_op jit(solution)/shard_map/while/body/eval_jaxpr/ppermute | solution.py:14
  625.6 5.2 collective-permute-start
  630.8 14.7 %collective-permute-done = bf16[1568,256]{1,0:T(8,128)(2,1)} collective-permute-done((bf16[1568,256]{1,0:T(8,128)(2,1)S(1)}, bf16[1568,256]{1,0:T(8,128)(2,1)}, u32[]{:S(2)}, u32[]{:S(2)}) %collective-permute-start) | collective-permute-done | bytes 802848 | tf_op jit(solution)/shard_map/while/body/eval_jaxpr/ppermute | solution.py:14
  649.5 5.2 collective-permute-start
  654.7 13.7 %collective-permute-done = bf16[1568,256]{1,0:T(8,128)(2,1)} collective-permute-done((bf16[1568,256]{1,0:T(8,128)(2,1)S(1)}, bf16[1568,256]{1,0:T(8,128)(2,1)}, u32[]{:S(2)}, u32[]{:S(2)}) %collective-permute-start) | collective-permute-done | bytes 802848 | tf_op jit(solution)/shard_map/while/body/eval_jaxpr/ppermute | solution.py:14
  672.5 5.2 collective-permute-start
  677.7 12.8 %collective-permute-done = bf16[1568,256]{1,0:T(8,128)(2,1)} collective-permute-done((bf16[1568,256]{1,0:T(8,128)(2,1)S(1)}, bf16[1568,256]{1,0:T(8,128)(2,1)}, u32[]{:S(2)}, u32[]{:S(2)}) %collective-permute-start) | collective-permute-done | bytes 802848 | tf_op jit(solution)/shard_map/while/body/eval_jaxpr/ppermute | solution.py:14
  694.6 5.2 collective-permute-start
  699.7 11.9 %collective-permute-done = bf16[1568,256]{1,0:T(8,128)(2,1)} collective-permute-done((bf16[1568,256]{1,0:T(8,128)(2,1)S(1)}, bf16[1568,256]{1,0:T(8,128)(2,1)}, u32[]{:S(2)}, u32[]{:S(2)}) %collective-permute-start) | collective-permute-done | bytes 802848 | tf_op jit(solution)/shard_map/while/body/eval_jaxpr/ppermute | solution.py:14
  715.7 5.8 collective-permute-start
  721.5 11.0 %collective-permute-done = bf16[1568,256]{1,0:T(8,128)(2,1)} collective-permute-done((bf16[1568,256]{1,0:T(8,128)(2,1)S(1)}, bf16[1568,256]{1,0:T(8,128)(2,1)}, u32[]{:S(2)}, u32[]{:S(2)}) %collective-permute-start) | collective-permute-done | bytes 802848 | tf_op jit(solution)/shard_map/while/body/eval_jaxpr/ppermute | solution.py:14
  736.6 7.3 collective-permute-start
  743.9 10.1 collective-permute-done
  758.0 7.3 collective-permute-start
  765.3 9.1 collective-permute-done
  778.5 7.3 collective-permute-start
  785.7 8.1 collective-permute-done
  797.9 7.3 collective-permute-start
  805.2 8.1 collective-permute-done
  817.4 7.3 collective-permute-start
  824.7 8.1 collective-permute-done
  836.9 7.3 collective-permute-start
  844.2 8.1 collective-permute-done
  856.4 7.4 collective-permute-start
  863.8 8.3 collective-permute-done
  876.2 7.3 collective-permute-start
  883.4 9.4 collective-permute-done
  896.9 7.6 collective-permute-start
  904.5 10.5 %collective-permute-done = bf16[1568,256]{1,0:T(8,128)(2,1)} collective-permute-done((bf16[1568,256]{1,0:T(8,128)(2,1)S(1)}, bf16[1568,256]{1,0:T(8,128)(2,1)}, u32[]{:S(2)}, u32[]{:S(2)}) %collective-permute-start) | collective-permute-done | bytes 802848 | tf_op jit(solution)/shard_map/while/body/eval_jaxpr/ppermute | solution.py:14
  917.4 4.3 multiply_convert_fusion.1
  921.7 4.5 convolution_convert_fusion
  926.2 92.4 %reduce-scatter.2.cloned.1.call-done = bf16[3136,256]{1,0:T(8,128)(2,1)} async-done(((bf16[3136,1024]{1,0:T(8,128)(2,1)}), bf16[3136,256]{1,0:T(8,128)(2,1)}) %reduce-scatter.2.cloned.1.call-update) | async-done | bytes 1605648 | tf_op jit(solution)/shard_map/reduce_scatter | solution.py:118
  1018.6 3.9 add_convert_fusion
  (85 shorter events, 89.4 us)
Async XLA Ops:
  6.5 16.3 %copy-start = (bf16[3,1024,256]{2,1,0:T(8,128)(2,1)S(1)}, bf16[3,1024,256]{2,1,0:T(8,128)(2,1)}, u32[]{:S(2)}) copy-start(bf16[3,1024,256]{2,1,0:T(8,128)(2,1)} %param.17) | copy-start | bytes 4718596
  6.5 527.9 %all-gather.3.cloned.1.call-start = ((), (), s32[]{:S(2)}) async-start(), calls=%async_computation.2 | async-start | bytes 32112640 | tf_op jit(solution)/shard_map/all_gather | solution.py:72
  173.3 15.7 %copy-start.3 = (bf16[2,1568,4,64]{1,0,3,2:T(2,128)(2,1)S(1)}, bf16[2,1568,4,64]{1,0,3,2:T(2,128)(2,1)}, u32[]{:S(2)}) copy-start(bf16[2,1568,4,64]{1,0,3,2:T(2,128)(2,1)} %get-tuple-element.146) | copy-start | bytes 4816900
  218.6 5.5 copy-start.2
  291.9 6.4 copy-start.4
  302.9 0.7 copy-start.7
  302.9 8.2 copy-start.6
  302.9 715.6 %reduce-scatter.2.cloned.1.call-start = ((), (), s32[]{:S(2)}) async-start(), calls=%async_computation.1 | async-start | bytes 8028160 | tf_op jit(solution)/shard_map/reduce_scatter | solution.py:118
  304.1 5.7 collective-permute-start.1
  601.9 19.6 %collective-permute-start = (bf16[1568,256]{1,0:T(8,128)(2,1)S(1)}, bf16[1568,256]{1,0:T(8,128)(2,1)}, u32[]{:S(2)}, u32[]{:S(2)}) collective-permute-start(bf16[1568,256]{1,0:T(8,128)(2,1)S(1)} %fusion.40), channel_id=1, source_target_pairs={{0,4},{4,8},{8,12},{12,16},{16,20},{20,24},{24,28},{28,32},{32,36}... | collective-permute-start | bytes 2408456 | tf_op jit(solution)/shard_map/while/body/eval_jaxpr/ppermute | solution.py:14
  625.6 19.8 %collective-permute-start = (bf16[1568,256]{1,0:T(8,128)(2,1)S(1)}, bf16[1568,256]{1,0:T(8,128)(2,1)}, u32[]{:S(2)}, u32[]{:S(2)}) collective-permute-start(bf16[1568,256]{1,0:T(8,128)(2,1)S(1)} %fusion.40), channel_id=1, source_target_pairs={{0,4},{4,8},{8,12},{12,16},{16,20},{20,24},{24,28},{28,32},{32,36}... | collective-permute-start | bytes 2408456 | tf_op jit(solution)/shard_map/while/body/eval_jaxpr/ppermute | solution.py:14
  649.5 18.9 %collective-permute-start = (bf16[1568,256]{1,0:T(8,128)(2,1)S(1)}, bf16[1568,256]{1,0:T(8,128)(2,1)}, u32[]{:S(2)}, u32[]{:S(2)}) collective-permute-start(bf16[1568,256]{1,0:T(8,128)(2,1)S(1)} %fusion.40), channel_id=1, source_target_pairs={{0,4},{4,8},{8,12},{12,16},{16,20},{20,24},{24,28},{28,32},{32,36}... | collective-permute-start | bytes 2408456 | tf_op jit(solution)/shard_map/while/body/eval_jaxpr/ppermute | solution.py:14
  672.5 18.0 %collective-permute-start = (bf16[1568,256]{1,0:T(8,128)(2,1)S(1)}, bf16[1568,256]{1,0:T(8,128)(2,1)}, u32[]{:S(2)}, u32[]{:S(2)}) collective-permute-start(bf16[1568,256]{1,0:T(8,128)(2,1)S(1)} %fusion.40), channel_id=1, source_target_pairs={{0,4},{4,8},{8,12},{12,16},{16,20},{20,24},{24,28},{28,32},{32,36}... | collective-permute-start | bytes 2408456 | tf_op jit(solution)/shard_map/while/body/eval_jaxpr/ppermute | solution.py:14
  694.6 17.1 %collective-permute-start = (bf16[1568,256]{1,0:T(8,128)(2,1)S(1)}, bf16[1568,256]{1,0:T(8,128)(2,1)}, u32[]{:S(2)}, u32[]{:S(2)}) collective-permute-start(bf16[1568,256]{1,0:T(8,128)(2,1)S(1)} %fusion.40), channel_id=1, source_target_pairs={{0,4},{4,8},{8,12},{12,16},{16,20},{20,24},{24,28},{28,32},{32,36}... | collective-permute-start | bytes 2408456 | tf_op jit(solution)/shard_map/while/body/eval_jaxpr/ppermute | solution.py:14
  715.7 16.8 %collective-permute-start = (bf16[1568,256]{1,0:T(8,128)(2,1)S(1)}, bf16[1568,256]{1,0:T(8,128)(2,1)}, u32[]{:S(2)}, u32[]{:S(2)}) collective-permute-start(bf16[1568,256]{1,0:T(8,128)(2,1)S(1)} %fusion.40), channel_id=1, source_target_pairs={{0,4},{4,8},{8,12},{12,16},{16,20},{20,24},{24,28},{28,32},{32,36}... | collective-permute-start | bytes 2408456 | tf_op jit(solution)/shard_map/while/body/eval_jaxpr/ppermute | solution.py:14
  736.6 17.3 %collective-permute-start = (bf16[1568,256]{1,0:T(8,128)(2,1)S(1)}, bf16[1568,256]{1,0:T(8,128)(2,1)}, u32[]{:S(2)}, u32[]{:S(2)}) collective-permute-start(bf16[1568,256]{1,0:T(8,128)(2,1)S(1)} %fusion.40), channel_id=1, source_target_pairs={{0,4},{4,8},{8,12},{12,16},{16,20},{20,24},{24,28},{28,32},{32,36}... | collective-permute-start | bytes 2408456 | tf_op jit(solution)/shard_map/while/body/eval_jaxpr/ppermute | solution.py:14
  758.0 16.4 %collective-permute-start = (bf16[1568,256]{1,0:T(8,128)(2,1)S(1)}, bf16[1568,256]{1,0:T(8,128)(2,1)}, u32[]{:S(2)}, u32[]{:S(2)}) collective-permute-start(bf16[1568,256]{1,0:T(8,128)(2,1)S(1)} %fusion.40), channel_id=1, source_target_pairs={{0,4},{4,8},{8,12},{12,16},{16,20},{20,24},{24,28},{28,32},{32,36}... | collective-permute-start | bytes 2408456 | tf_op jit(solution)/shard_map/while/body/eval_jaxpr/ppermute | solution.py:14
  778.5 15.4 %collective-permute-start = (bf16[1568,256]{1,0:T(8,128)(2,1)S(1)}, bf16[1568,256]{1,0:T(8,128)(2,1)}, u32[]{:S(2)}, u32[]{:S(2)}) collective-permute-start(bf16[1568,256]{1,0:T(8,128)(2,1)S(1)} %fusion.40), channel_id=1, source_target_pairs={{0,4},{4,8},{8,12},{12,16},{16,20},{20,24},{24,28},{28,32},{32,36}... | collective-permute-start | bytes 2408456 | tf_op jit(solution)/shard_map/while/body/eval_jaxpr/ppermute | solution.py:14
  797.9 15.4 %collective-permute-start = (bf16[1568,256]{1,0:T(8,128)(2,1)S(1)}, bf16[1568,256]{1,0:T(8,128)(2,1)}, u32[]{:S(2)}, u32[]{:S(2)}) collective-permute-start(bf16[1568,256]{1,0:T(8,128)(2,1)S(1)} %fusion.40), channel_id=1, source_target_pairs={{0,4},{4,8},{8,12},{12,16},{16,20},{20,24},{24,28},{28,32},{32,36}... | collective-permute-start | bytes 2408456 | tf_op jit(solution)/shard_map/while/body/eval_jaxpr/ppermute | solution.py:14
  817.4 15.4 %collective-permute-start = (bf16[1568,256]{1,0:T(8,128)(2,1)S(1)}, bf16[1568,256]{1,0:T(8,128)(2,1)}, u32[]{:S(2)}, u32[]{:S(2)}) collective-permute-start(bf16[1568,256]{1,0:T(8,128)(2,1)S(1)} %fusion.40), channel_id=1, source_target_pairs={{0,4},{4,8},{8,12},{12,16},{16,20},{20,24},{24,28},{28,32},{32,36}... | collective-permute-start | bytes 2408456 | tf_op jit(solution)/shard_map/while/body/eval_jaxpr/ppermute | solution.py:14
  836.9 15.4 %collective-permute-start = (bf16[1568,256]{1,0:T(8,128)(2,1)S(1)}, bf16[1568,256]{1,0:T(8,128)(2,1)}, u32[]{:S(2)}, u32[]{:S(2)}) collective-permute-start(bf16[1568,256]{1,0:T(8,128)(2,1)S(1)} %fusion.40), channel_id=1, source_target_pairs={{0,4},{4,8},{8,12},{12,16},{16,20},{20,24},{24,28},{28,32},{32,36}... | collective-permute-start | bytes 2408456 | tf_op jit(solution)/shard_map/while/body/eval_jaxpr/ppermute | solution.py:14
  856.4 15.7 %collective-permute-start = (bf16[1568,256]{1,0:T(8,128)(2,1)S(1)}, bf16[1568,256]{1,0:T(8,128)(2,1)}, u32[]{:S(2)}, u32[]{:S(2)}) collective-permute-start(bf16[1568,256]{1,0:T(8,128)(2,1)S(1)} %fusion.40), channel_id=1, source_target_pairs={{0,4},{4,8},{8,12},{12,16},{16,20},{20,24},{24,28},{28,32},{32,36}... | collective-permute-start | bytes 2408456 | tf_op jit(solution)/shard_map/while/body/eval_jaxpr/ppermute | solution.py:14
  876.2 16.7 %collective-permute-start = (bf16[1568,256]{1,0:T(8,128)(2,1)S(1)}, bf16[1568,256]{1,0:T(8,128)(2,1)}, u32[]{:S(2)}, u32[]{:S(2)}) collective-permute-start(bf16[1568,256]{1,0:T(8,128)(2,1)S(1)} %fusion.40), channel_id=1, source_target_pairs={{0,4},{4,8},{8,12},{12,16},{16,20},{20,24},{24,28},{28,32},{32,36}... | collective-permute-start | bytes 2408456 | tf_op jit(solution)/shard_map/while/body/eval_jaxpr/ppermute | solution.py:14
  896.9 18.1 %collective-permute-start = (bf16[1568,256]{1,0:T(8,128)(2,1)S(1)}, bf16[1568,256]{1,0:T(8,128)(2,1)}, u32[]{:S(2)}, u32[]{:S(2)}) collective-permute-start(bf16[1568,256]{1,0:T(8,128)(2,1)S(1)} %fusion.40), channel_id=1, source_target_pairs={{0,4},{4,8},{8,12},{12,16},{16,20},{20,24},{24,28},{28,32},{32,36}... | collective-permute-start | bytes 2408456 | tf_op jit(solution)/shard_map/while/body/eval_jaxpr/ppermute | solution.py:14
  917.4 4.3 copy-start.5
  926.2 96.3 %copy-start.1 = (bf16[3,1024,256]{2,1,0:T(8,128)(2,1)S(1)}, bf16[3,1024,256]{2,1,0:T(8,128)(2,1)}, u32[]{:S(2)}) copy-start(bf16[3,1024,256]{2,1,0:T(8,128)(2,1)} %param.17) | copy-start | bytes 4718596
Sparse Core Ops, SparseCore 0:
  303.1 231.3 all-gather.2
  926.3 92.2 reduce-scatter.1
